TPU v7x, 256 devices: a whole 4x4x8 slice. The times are simulated.
256 devices in a mesh: rows: 16 (over y, x), cols: 8 (over z), depth: 2 (over core).
Axes of the slice: x: 4, y: 4, z: 8, core: 2. Of those that a mesh axis runs over, the one named last changes fastest.
Arguments:
- tile_left: float32 [16, 8, 64, 2048], P('rows', 'cols'), may hold values from -6 to 6
- tile_right: float32 [16, 8, 64, 2048], P('rows', 'cols'), may hold values from -0.75 to 0.75
- left_u: bfloat16 [2, 16, 16, 64, 2048], P('depth', 'cols', 'rows'), may hold values from -6 to 6
- left_v: bfloat16 [2, 16, 16, 64, 2048], P('depth', 'cols', 'rows'), may hold values from -0.0625 to 0.0625
- rank_left: int32 [2, 16, 16], P('depth', 'cols', 'rows'), may hold values from 16 to 64
- right_u: bfloat16 [2, 16, 8, 64, 2048], P('depth', 'rows', 'cols'), may hold values from -6 to 6
- right_v: bfloat16 [2, 16, 8, 64, 2048], P('depth', 'rows', 'cols'), may hold values from -0.0625 to 0.0625
- rank_right: int32 [2, 16, 8], P('depth', 'rows', 'cols'), may hold values from 16 to 64
- triples: int32 [16, 8, 2, 6], P('rows', 'cols', 'depth'), may hold values from -1 to 15, as said below
Outputs:
- new_left: float32 [16, 8, 64, 2048], P('rows', 'cols', None, 'depth')
- new_right: float32 [16, 8, 64, 2048], P('rows', 'cols', None, 'depth')
Inputs may be any that keep to these rules, and one draw needn't show every extreme that they name: `triples`: for each tile and layer the first entries are distinct panel numbers of 0 to 15 and the remaining entries are -1; every list has at least one panel number, and in every draw some tile in some layer lists all 6.
All inputs are finite; a program needn't handle non-finite values.
Results may differ from a plain program's by a relative error of at most 0.0043.
Values may be sent and summed in bfloat16 or wider, within the bound.
No kernel may reach another device: no remote copies, remote signals or barrier semaphores. Data moves between devices by JAX's collectives and lax.ppermute only.
A program may use at most 128 MiB of HBM per device.

v0:
```python
import math
import jax
import jax.numpy as jnp
from jax import lax
from jax.sharding import PartitionSpec as P

NB = 2048
RK = 64
HIGHEST = lax.Precision.HIGHEST


def swapped(block, axis, apart):
    count = lax.axis_size(axis)
    route = []
    for low in range(count):
        high = low | 1 << apart
        if high != low and high < count:
            route += [(low, high), (high, low)]
    return lax.ppermute(block, axis, route)


def cross(first, second, dim_first, dim_second):
    return lax.dot_general(
        first,
        second,
        (((dim_first,), (dim_second,)), ((), ())),
        precision=HIGHEST,
        preferred_element_type=jnp.float32,
    )


def start_rows(rank, width):
    freq = lax.broadcasted_iota(jnp.int32, (rank, width), 0) + 1
    cell = 2 * lax.broadcasted_iota(jnp.int32, (rank, width), 1) + 1
    phase = freq * cell % (4 * width)
    return jnp.cos(phase.astype(jnp.float32) * (math.pi / (2 * width)))


def orthonormal(rows_t):
    gram = cross(rows_t, rows_t, 1, 1)
    shift = 1e-05 * jnp.trace(gram) / gram.shape[0] + 1e-06
    gram = gram + shift * jnp.eye(gram.shape[0], dtype=gram.dtype)
    lower = lax.linalg.cholesky(gram)
    return lax.linalg.triangular_solve(lower, rows_t, left_side=True, lower=True)


def compress(left_t, right_t):
    probe = start_rows(RK, NB)
    for sweep in range(2):
        first = cross(left_t, probe, 1, 1)
        image = orthonormal(cross(first, right_t, 0, 0))
        second = cross(right_t, image, 1, 1)
        probe = orthonormal(cross(second, left_t, 0, 0))
    first = cross(left_t, probe, 1, 1)
    return (probe, cross(first, right_t, 0, 0))


def slot_term(outer_left, inner_left, rank_l, inner_right, rank_r):
    inner = lax.dot_general(
        inner_left, inner_right, (((1,), (1,)), ((), ())), preferred_element_type=jnp.float32
    )
    index = jnp.arange(RK)
    keep = (index[:, None] < rank_l) & (index[None, :] < rank_r)
    inner = jnp.where(keep, inner, 0.0).astype(jnp.bfloat16)
    return -lax.dot_general(
        inner, outer_left, (((0,), (0,)), ((), ())), preferred_element_type=jnp.float32
    )


def shards(tile_left, tile_right, left_u, left_v, rank_left, right_u, right_v, rank_right, triples):
    layers = lax.axis_size("depth")
    tcols = tile_left.shape[1]
    slots = triples.shape[3]
    row_u, row_v, row_rank = (
        lax.all_gather(left_u, "cols", axis=1, tiled=True),
        lax.all_gather(left_v, "cols", axis=1, tiled=True),
        lax.all_gather(rank_left, "cols", axis=1, tiled=True),
    )
    col_u, col_v, col_rank = (
        lax.all_gather(right_u, "rows", axis=1, tiled=True),
        lax.all_gather(right_v, "rows", axis=1, tiled=True),
        lax.all_gather(rank_right, "rows", axis=1, tiled=True),
    )
    term_list = []
    base_list = []
    tile = 0
    for slot in range(slots):
        panel = triples[0, tile, 0, slot]
        valid = panel >= 0
        chosen = jnp.maximum(panel, 0)
        term_list.append(
            lax.cond(
                valid,
                lambda: slot_term(
                    row_u[0, chosen, 0],
                    row_v[0, chosen, 0],
                    row_rank[0, chosen, 0],
                    col_v[0, chosen, tile],
                    col_rank[0, chosen, tile],
                ),
                lambda: jnp.zeros((RK, NB), jnp.float32),
            )
        )
        base_list.append(
            jnp.where(valid, col_u[0, chosen, tile], jnp.zeros((RK, NB), jnp.bfloat16))
        )
    terms = jnp.stack(term_list).reshape(tcols, slots, RK, NB)
    bases = jnp.stack(base_list).reshape(tcols, slots, RK, NB)
    probes = []
    images = []
    tile = 0
    left_t = jnp.concatenate(
        [tile_left[0, tile] / layers, terms[tile].reshape(slots * RK, NB)], axis=0
    )
    right_t = jnp.concatenate(
        [tile_right[0, tile], bases[tile].astype(jnp.float32).reshape(slots * RK, NB)], axis=0
    )
    probe, image = compress(left_t, right_t)
    probes.append(probe)
    images.append(image)
    probes = jnp.stack(probes)
    images = jnp.stack(images)
    layer_index = lax.axis_index("depth")
    other_probes, other_images = swapped((probes, images), "depth", 0)
    lower_side = layer_index >> 0 & 1 == 0
    first_probes = jnp.where(lower_side, probes, other_probes)
    second_probes = jnp.where(lower_side, other_probes, probes)
    first_images = jnp.where(lower_side, images, other_images)
    second_images = jnp.where(lower_side, other_images, images)
    tile = 0
    probe, image = compress(
        jnp.concatenate([first_probes[tile], second_probes[tile]], axis=0),
        jnp.concatenate([first_images[tile], second_images[tile]], axis=0),
    )
    joined_probes = [probe]
    joined_images = [image]
    probes = jnp.stack(joined_probes)
    images = jnp.stack(joined_images)
    share = NB // layers
    offset = layer_index * share
    new_left = lax.dynamic_slice_in_dim(probes * math.sqrt(NB), offset, share, 2).reshape(
        1, tcols, RK, share
    )
    new_right = lax.dynamic_slice_in_dim(images / math.sqrt(NB), offset, share, 2).reshape(
        1, tcols, RK, share
    )
    return (new_left, new_right)


def solution(mesh):
    in_specs = (
        P("rows", "cols", None, None),
        P("rows", "cols", None, None),
        P("depth", "cols", "rows", None, None),
        P("depth", "cols", "rows", None, None),
        P("depth", "cols", "rows"),
        P("depth", "rows", "cols", None, None),
        P("depth", "rows", "cols", None, None),
        P("depth", "rows", "cols"),
        P("rows", "cols", "depth", None),
    )
    out_specs = (P("rows", "cols", None, "depth"), P("rows", "cols", None, "depth"))
    return jax.shard_map(shards, mesh=mesh, in_specs=in_specs, out_specs=out_specs, check_vma=False)
```

profile of v0, /device:TPU:57, one launch (start us, length us, event | category | flops | bytes accessed | tf_op | source)
XLA Modules:
  0.0 460.7 jit_solution(14910221890863665000)
XLA Ops:
  12.6 10.3 %all-reduce.1 = s32[16]{0:T(128)S(1)} all-reduce(s32[16]{0:T(128)S(1)} %bitcast_dynamic-update-slice_fusion.6), channel_id=1, replica_groups=mesh['rows'=16,'cols'=8,'depth'=2] {'rows'}, use_global_device_ids=true, to_apply=%add.1 | all-reduce | flops 16 | bytes 128
  34.9 13.5 %all-reduce = s32[16]{0:T(128)S(1)} all-reduce(s32[16]{0:T(128)S(1)} %bitcast_dynamic-update-slice_fusion.7), channel_id=1, replica_groups=mesh['rows'=16,'cols'=8,'depth'=2] {'cols'}, use_global_device_ids=true, to_apply=%add | all-reduce | flops 16 | bytes 128
  50.2 15.1 %all-gather.5.cloned.1.call-done = bf16[1,16,1,64,2048]{4,3,2,0,1:T(8,128)(2,1)} async-done(((bf16[1,2,1,64,2048]{4,3,2,0,1:T(8,128)(2,1)}), bf16[1,16,1,64,2048]{4,3,2,0,1:T(8,128)(2,1)}) %all-gather.5.cloned.1.call-update) | async-done | bytes 4194320 | tf_op jit(solution)/shard_map/all_gather | solution.py:76
  65.3 55.2 %all-gather.9.cloned.1.call-done = bf16[1,16,1,64,2048]{4,3,2,0,1:T(8,128)(2,1)} async-done(((bf16[1,2,1,64,2048]{4,3,2,0,1:T(8,128)(2,1)}), bf16[1,16,1,64,2048]{4,3,2,0,1:T(8,128)(2,1)}) %all-gather.9.cloned.1.call-update) | async-done | bytes 4194320 | tf_op jit(solution)/shard_map/all_gather | solution.py:75
  120.4 59.2 %all-gather.7.cloned.1.call-done = bf16[1,16,1,64,2048]{4,3,2,0,1:T(8,128)(2,1)} async-done(((bf16[1,1,1,64,2048]{4,3,2,0,1:T(8,128)(2,1)}), bf16[1,16,1,64,2048]{4,3,2,0,1:T(8,128)(2,1)}) %all-gather.7.cloned.1.call-update) | async-done | bytes 4194320 | tf_op jit(solution)/shard_map/all_gather | solution.py:81
  184.0 54.2 %all-gather.11.cloned.1.call-done = bf16[1,16,1,64,2048]{4,3,2,0,1:T(8,128)(2,1)} async-done(((bf16[1,1,1,64,2048]{4,3,2,0,1:T(8,128)(2,1)}), bf16[1,16,1,64,2048]{4,3,2,0,1:T(8,128)(2,1)}) %all-gather.11.cloned.1.call-update) | async-done | bytes 4194320 | tf_op jit(solution)/shard_map/all_gather | solution.py:80
  276.7 6.9 %fusion.122 = f32[448,64]{1,0:T(8,128)S(1)} fusion(f32[384,2048]{1,0:T(8,128)} %bitcast.304, f32[64,2048]{1,0:T(8,128)} %multiply_bitcast_fusion, s32[2048]{0:T(1024)S(1)} %multiply_add_fusion, s32[64]{0:T(128)S(1)} %iota_add_fusion), kind=kOutput, calls=%fused_computation.132 | convolution fusion | flops 707395584 | bytes 3793152 | tf_op jit(solution)/shard_map/dot_general | solution.py:23
  288.7 5.8 %custom-call.20 = f32[64,64]{1,0:T(8,128)S(1)} custom-call(f32[64,64]{1,0:T(8,128)S(1)} %fusion.180), custom_call_target="Cholesky" | custom-call | tf_op jit(solution)/shard_map/cholesky/custom-call.1 | solution.py:43
  295.9 4.9 %custom-call.21 = f32[1,64,64]{1,2,0:T(8,128)S(1)} custom-call(f32[1,64,64]{2,1,0:T(8,128)S(1)} %fusion.141), custom_call_target="InvertDiagBlocksLowerTriangular" | custom-call | tf_op jit(solution)/shard_map/triangular_solve/custom-call.0 | solution.py:44
  312.0 5.8 %custom-call.22 = f32[64,64]{1,0:T(8,128)S(1)} custom-call(f32[64,64]{1,0:T(8,128)S(1)} %fusion.176), custom_call_target="Cholesky" | custom-call | tf_op jit(solution)/shard_map/cholesky/custom-call.1 | solution.py:43
  319.2 4.9 %custom-call.23 = f32[1,64,64]{1,2,0:T(8,128)S(1)} custom-call(f32[1,64,64]{2,1,0:T(8,128)S(1)} %fusion.142), custom_call_target="InvertDiagBlocksLowerTriangular" | custom-call | tf_op jit(solution)/shard_map/triangular_solve/custom-call.0 | solution.py:44
  325.9 5.0 %fusion.120 = f32[448,64]{1,0:T(8,128)S(1)} fusion(f32[64,2048]{1,0:T(8,128)S(1)} %fusion.173, f32[384,2048]{1,0:T(8,128)} %bitcast.305, f32[64,2048]{1,0:T(8,128)} %multiply_bitcast_fusion), kind=kOutput, calls=%fused_computation.130 | convolution fusion | flops 705560576 | bytes 4308992 | tf_op jit(solution)/shard_map/dot_general | solution.py:23
  336.0 6.2 %custom-call.24 = f32[64,64]{1,0:T(8,128)S(1)} custom-call(f32[64,64]{1,0:T(8,128)S(1)} %fusion.172), custom_call_target="Cholesky" | custom-call | tf_op jit(solution)/shard_map/cholesky/custom-call.1 | solution.py:43
  343.6 4.9 %custom-call.25 = f32[1,64,64]{1,2,0:T(8,128)S(1)} custom-call(f32[1,64,64]{2,1,0:T(8,128)S(1)} %fusion.143), custom_call_target="InvertDiagBlocksLowerTriangular" | custom-call | tf_op jit(solution)/shard_map/triangular_solve/custom-call.0 | solution.py:44
  359.5 5.8 %custom-call.26 = f32[64,64]{1,0:T(8,128)S(1)} custom-call(f32[64,64]{1,0:T(8,128)S(1)} %fusion.168), custom_call_target="Cholesky" | custom-call | tf_op jit(solution)/shard_map/cholesky/custom-call.1 | solution.py:43
  366.7 4.9 %custom-call.27 = f32[1,64,64]{1,2,0:T(8,128)S(1)} custom-call(f32[1,64,64]{2,1,0:T(8,128)S(1)} %fusion.144), custom_call_target="InvertDiagBlocksLowerTriangular" | custom-call | tf_op jit(solution)/shard_map/triangular_solve/custom-call.0 | solution.py:44
  374.1 5.2 %fusion.118 = f32[448,64]{1,0:T(8,128)S(1)} fusion(f32[64,2048]{1,0:T(8,128)} %fusion.165, f32[384,2048]{1,0:T(8,128)} %bitcast.306, f32[64,2048]{1,0:T(8,128)} %multiply_bitcast_fusion), kind=kOutput, calls=%fused_computation.128 | convolution fusion | flops 705560576 | bytes 4308992 | tf_op jit(solution)/shard_map/dot_general | solution.py:23
  389.5 5.8 %custom-call.28 = f32[64,64]{1,0:T(8,128)S(1)} custom-call(f32[64,64]{1,0:T(8,128)S(1)} %fusion.164), custom_call_target="Cholesky" | custom-call | tf_op jit(solution)/shard_map/cholesky/custom-call.1 | solution.py:43
  396.7 4.9 %custom-call.29 = f32[1,64,64]{1,2,0:T(8,128)S(1)} custom-call(f32[1,64,64]{2,1,0:T(8,128)S(1)} %fusion.145), custom_call_target="InvertDiagBlocksLowerTriangular" | custom-call | tf_op jit(solution)/shard_map/triangular_solve/custom-call.0 | solution.py:44
  405.8 5.8 %custom-call.30 = f32[64,64]{1,0:T(8,128)S(1)} custom-call(f32[64,64]{1,0:T(8,128)S(1)} %fusion.160), custom_call_target="Cholesky" | custom-call | tf_op jit(solution)/shard_map/cholesky/custom-call.1 | solution.py:43
  413.0 4.9 %custom-call.31 = f32[1,64,64]{1,2,0:T(8,128)S(1)} custom-call(f32[1,64,64]{2,1,0:T(8,128)S(1)} %fusion.146), custom_call_target="InvertDiagBlocksLowerTriangular" | custom-call | tf_op jit(solution)/shard_map/triangular_solve/custom-call.0 | solution.py:44
  422.3 5.8 %custom-call.32 = f32[64,64]{1,0:T(8,128)S(1)} custom-call(f32[64,64]{1,0:T(8,128)S(1)} %fusion.156), custom_call_target="Cholesky" | custom-call | tf_op jit(solution)/shard_map/cholesky/custom-call.1 | solution.py:43
  429.5 4.9 %custom-call.33 = f32[1,64,64]{1,2,0:T(8,128)S(1)} custom-call(f32[1,64,64]{2,1,0:T(8,128)S(1)} %fusion.147), custom_call_target="InvertDiagBlocksLowerTriangular" | custom-call | tf_op jit(solution)/shard_map/triangular_solve/custom-call.0 | solution.py:44
  438.7 5.8 %custom-call.34 = f32[64,64]{1,0:T(8,128)S(1)} custom-call(f32[64,64]{1,0:T(8,128)S(1)} %fusion.152), custom_call_target="Cholesky" | custom-call | tf_op jit(solution)/shard_map/cholesky/custom-call.1 | solution.py:43
  (164 shorter events, 151.3 us)
Async XLA Ops:
  7.2 58.1 %all-gather.5.cloned.1.call-start = ((), (), s32[]{:S(2)}) async-start(), calls=%async_computation | async-start | bytes 4718592 | tf_op jit(solution)/shard_map/all_gather | solution.py:76
  7.9 112.5 %all-gather.9.cloned.1.call-start = ((), (), s32[]{:S(2)}) async-start(), calls=%async_computation.2 | async-start | bytes 4718592 | tf_op jit(solution)/shard_map/all_gather | solution.py:75
  8.6 171.0 %all-gather.7.cloned.1.call-start = ((), (), s32[]{:S(2)}) async-start(), calls=%async_computation.1 | async-start | bytes 4456448 | tf_op jit(solution)/shard_map/all_gather | solution.py:81
  9.4 228.8 %all-gather.11.cloned.1.call-start = ((), (), s32[]{:S(2)}) async-start(), calls=%async_computation.3 | async-start | bytes 4456448 | tf_op jit(solution)/shard_map/all_gather | solution.py:80
  274.7 8.8 %copy-start.2 = (f32[1,1,64,2048]{3,2,1,0:T(8,128)S(1)}, f32[1,1,64,2048]{3,2,1,0:T(8,128)}, u32[]{:S(2)}) copy-start(f32[1,1,64,2048]{3,2,1,0:T(8,128)} %param.25) | copy-start | bytes 1572868
  286.0 0.8 copy-start.7
  300.8 6.1 %copy-start = (f32[6,64,2048]{2,1,0:T(8,128)S(1)}, f32[6,64,2048]{2,1,0:T(8,128)}, u32[]{:S(2)}) copy-start(f32[6,64,2048]{2,1,0:T(8,128)} %constant_dynamic-update-slice_fusion) | copy-start | bytes 9437188
  300.8 6.1 %copy-start.5 = (f32[64,2048]{1,0:T(8,128)S(1)}, f32[64,2048]{1,0:T(8,128)}, u32[]{:S(2)}) copy-start(f32[64,2048]{1,0:T(8,128)} %multiply_bitcast_fusion) | copy-start | bytes 1572868
  309.3 0.8 copy-start.8
  324.1 6.7 %copy-start.3 = (f32[1,1,64,2048]{3,2,1,0:T(8,128)S(1)}, f32[1,1,64,2048]{3,2,1,0:T(8,128)}, u32[]{:S(2)}) copy-start(f32[1,1,64,2048]{3,2,1,0:T(8,128)} %param.25) | copy-start | bytes 1572868
  333.3 0.8 copy-start.9
  348.5 5.9 %copy-start.1 = (f32[6,64,2048]{2,1,0:T(8,128)S(1)}, f32[6,64,2048]{2,1,0:T(8,128)}, u32[]{:S(2)}) copy-start(f32[6,64,2048]{2,1,0:T(8,128)} %constant_dynamic-update-slice_fusion) | copy-start | bytes 9437188
  348.5 5.9 %copy-start.6 = (f32[64,2048]{1,0:T(8,128)S(1)}, f32[64,2048]{1,0:T(8,128)}, u32[]{:S(2)}) copy-start(f32[64,2048]{1,0:T(8,128)} %multiply_bitcast_fusion) | copy-start | bytes 1572868
  356.8 0.8 copy-start.10
  374.1 8.4 %collective-permute-start.1 = (f32[1,64,2048]{2,1,0:T(8,128)}, f32[1,64,2048]{2,1,0:T(8,128)}, u32[]{:S(2)}, u32[]{:S(2)}) collective-permute-start(f32[1,64,2048]{2,1,0:T(8,128)} %bitcast.107), channel_id=1, source_target_pairs={{0,1},{1,0},{2,3},{3,2},{4,5},{5,4},{6,7},{7,6},{8,9},{9,8},{10,11... | collective-permute-start | bytes 1572872 | tf_op jit(solution)/shard_map/ppermute | solution.py:19
  374.1 5.2 %copy-start.4 = (f32[1,1,64,2048]{3,2,1,0:T(8,128)S(1)}, f32[1,1,64,2048]{3,2,1,0:T(8,128)}, u32[]{:S(2)}) copy-start(f32[1,1,64,2048]{3,2,1,0:T(8,128)} %param.25) | copy-start | bytes 1572868
  381.7 5.0 %collective-permute-start = (f32[1,64,2048]{2,1,0:T(8,128)S(1)}, f32[1,64,2048]{2,1,0:T(8,128)S(1)}, u32[]{:S(2)}, u32[]{:S(2)}) collective-permute-start(f32[1,64,2048]{2,1,0:T(8,128)S(1)} %convolution_bitcast_fusion), channel_id=1, source_target_pairs={{0,1},{1,0},{2,3},{3,2},{4,5},{5,4},{6,7},{7,6},{8,9},{9,8},{10,11... | collective-permute-start | bytes 1572872 | tf_op jit(solution)/shard_map/ppermute | solution.py:19
Sparse Core Ops, SparseCore 0:
  9.8 55.4 all-gather.4
  67.1 53.3 all-gather.8
  122.9 56.7 all-gather.6
  182.0 56.1 all-gather.10
where the time goes:
time: 466 us; the launch traced here: 461 us
  waiting for transfers between devices  186 us (40%)
  other arithmetic  115 us (25%)
  matrix products  81.8 us (18%)
  between operations  29 us (6%)
  blocking collectives  23.8 us (5%)
  local copies, waits for them, and re-layouts  23.2 us (5%)
    all_gather x1, waiting for transfers between devices, shards(): lax.all_gather(right_v, 'rows', axis=1, tiled=True)  59.2 us
    dot_general x28, matrix products, cross(): lax.dot_general(first, second, (((dim_first,), (dim_second,)), ((), ())),...  57.2 us
    all_gather x1, waiting for transfers between devices, shards(): lax.all_gather(left_u, 'cols', axis=1, tiled=True)  55.2 us
    all_gather x1, waiting for transfers between devices, shards(): lax.all_gather(right_u, 'rows', axis=1, tiled=True)  54.2 us
    another operation x24, other arithmetic, orthonormal(): lower = lax.linalg.cholesky(gram)  52.5 us
    another operation x16, other arithmetic, orthonormal(): lax.linalg.triangular_solve(lower, rows_t, left_side=True, lower=True)  44.4 us
    unnamed x2, blocking collectives  23.8 us
    unnamed x33, local copies, waits for them, and re-layouts  15.5 us
  transfers between devices with their start and end apart: 6, of which 4 were waited for; matrix products, arithmetic and copies ran while one was open for 5% of the time, Pallas kernels for 0%

commit v1 on v0

--- a/solution.py
+++ b/solution.py
@@ -71,8 +71,18 @@
     layers = lax.axis_size("depth")
     tcols = tile_left.shape[1]
     slots = triples.shape[3]
+
+    def treat_side_now(vals):
+        bank = []
+        for _ in range(lax.axis_size("cols")):
+            bank.append(vals)
+        met_up = jnp.stack(bank)
+        placed = lax.all_to_all(met_up, split_axis=0, concat_axis=0, axis_name="cols")
+        near = jnp.concatenate(placed, axis=1)
+        return near
+
     row_u, row_v, row_rank = (
-        lax.all_gather(left_u, "cols", axis=1, tiled=True),
+        treat_side_now(left_u),
         lax.all_gather(left_v, "cols", axis=1, tiled=True),
         lax.all_gather(rank_left, "cols", axis=1, tiled=True),
     )

time: 466 us -> 498 us (1.069)
  blocking collectives: 23.8 us -> 126 us
  waiting for transfers between devices: 186 us -> 109 us
  starting transfers between devices: 0.92 us -> 9.03 us
    unnamed x2, blocking collectives: 23.8 us -> 126 us
    all_gather x1 -> x0, waiting for transfers between devices: 55.2 us -> none  [shards(): lax.all_gather(left_u, 'cols', axis=1, tiled=True)]
    all_gather x1, waiting for transfers between devices: 15.1 us -> 0.01 us  [shards(): lax.all_gather(left_v, 'cols', axis=1, tiled=True)]
    all_to_all x0 -> x1, starting transfers between devices: none -> 8.15 us  [treat_side_now(): lax.all_to_all(met_up, split_axis=0, concat_axis=0, axis_name='cols')]
    all_gather x1, waiting for transfers between devices: 59.2 us -> 52.7 us  [shards(): lax.all_gather(right_v, 'rows', axis=1, tiled=True)]
    unnamed x33 -> x43, local copies, waits for them, and re-layouts: 15.5 us -> 13.5 us
  transfers between devices with their start and end apart: 6 -> 6, of which waited for: 4 -> 2; matrix products, arithmetic and copies ran while one was open for 5% -> 5% of each run, Pallas kernels for 0% -> 0%
where the time goes in v1:
time: 498 us; the launch traced here: 493 us
  blocking collectives  126 us (25%)
  other arithmetic  114 us (23%)
  waiting for transfers between devices  109 us (22%)
  matrix products  81.5 us (16%)
  between operations  29.1 us (6%)
  local copies, waits for them, and re-layouts  23.8 us (5%)
  starting transfers between devices  9.03 us (2%)
    unnamed x2, blocking collectives  126 us
    dot_general x28, matrix products, cross(): lax.dot_general(first, second, (((dim_first,), (dim_second,)), ((), ())),...  57.1 us
    all_gather x1, waiting for transfers between devices, shards(): lax.all_gather(right_u, 'rows', axis=1, tiled=True)  54.3 us
    all_gather x1, waiting for transfers between devices, shards(): lax.all_gather(right_v, 'rows', axis=1, tiled=True)  52.7 us
    another operation x24, other arithmetic, orthonormal(): lower = lax.linalg.cholesky(gram)  52.5 us
    another operation x16, other arithmetic, orthonormal(): lax.linalg.triangular_solve(lower, rows_t, left_side=True, lower=True)  44.4 us
    dot_general x6, matrix products, slot_term(): lax.dot_general(inner, outer_left, (((0,), (0,)), ((), ())), preferred_el...  14 us
    unnamed x43, local copies, waits for them, and re-layouts  13.5 us
  transfers between devices with their start and end apart: 6, of which 2 were waited for; matrix products, arithmetic and copies ran while one was open for 5% of the time, Pallas kernels for 0%

profile of v1, /device:TPU:57, one launch (start us, length us, event | category | flops | bytes accessed | tf_op | source)
XLA Modules:
  0.0 492.9 jit_solution(12095099587616378156)
XLA Ops:
  12.9 8.2 %all-to-all-start = ((bf16[8,1,2,1,64,2048]{5,4,2,3,1,0:T(8,128)(2,1)}), bf16[8,1,2,1,64,2048]{5,4,2,3,1,0:T(8,128)(2,1)}, u32[]{:S(2)}, u32[]{:S(2)}) async-start(bf16[8,1,2,1,64,2048]{5,4,2,3,1,0:T(8,128)(2,1)} %stack.73), calls=%async_computation | async-start | bytes 8388608 | tf_op jit(solution)/shard_map/all_to_all | solution.py:80
  23.0 11.6 %all-reduce.1 = s32[16]{0:T(128)S(1)} all-reduce(s32[16]{0:T(128)S(1)} %bitcast_dynamic-update-slice_fusion.6), channel_id=1, replica_groups=mesh['rows'=16,'cols'=8,'depth'=2] {'rows'}, use_global_device_ids=true, to_apply=%add.1 | all-reduce | flops 16 | bytes 128
  44.5 113.9 %all-reduce = s32[16]{0:T(128)S(1)} all-reduce(s32[16]{0:T(128)S(1)} %bitcast_dynamic-update-slice_fusion.7), channel_id=1, replica_groups=mesh['rows'=16,'cols'=8,'depth'=2] {'cols'}, use_global_device_ids=true, to_apply=%add | all-reduce | flops 16 | bytes 128
  159.2 52.7 %all-gather.6.cloned.1.call-done = bf16[1,16,1,64,2048]{4,3,2,0,1:T(8,128)(2,1)} async-done(((bf16[1,1,1,64,2048]{4,3,2,0,1:T(8,128)(2,1)}), bf16[1,16,1,64,2048]{4,3,2,0,1:T(8,128)(2,1)}) %all-gather.6.cloned.1.call-update) | async-done | bytes 4194320 | tf_op jit(solution)/shard_map/all_gather | solution.py:91
  216.3 54.3 %all-gather.8.cloned.1.call-done = bf16[1,16,1,64,2048]{4,3,2,0,1:T(8,128)(2,1)} async-done(((bf16[1,1,1,64,2048]{4,3,2,0,1:T(8,128)(2,1)}), bf16[1,16,1,64,2048]{4,3,2,0,1:T(8,128)(2,1)}) %all-gather.8.cloned.1.call-update) | async-done | bytes 4194320 | tf_op jit(solution)/shard_map/all_gather | solution.py:90
  309.0 6.8 %fusion.122 = f32[448,64]{1,0:T(8,128)S(1)} fusion(f32[384,2048]{1,0:T(8,128)} %bitcast.305, f32[64,2048]{1,0:T(8,128)} %multiply_bitcast_fusion, s32[2048]{0:T(1024)S(1)} %multiply_add_fusion, s32[64]{0:T(128)S(1)} %iota_add_fusion), kind=kOutput, calls=%fused_computation.132 | convolution fusion | flops 707395584 | bytes 3793152 | tf_op jit(solution)/shard_map/dot_general | solution.py:23
  321.0 5.8 %custom-call.20 = f32[64,64]{1,0:T(8,128)S(1)} custom-call(f32[64,64]{1,0:T(8,128)S(1)} %fusion.180), custom_call_target="Cholesky" | custom-call | tf_op jit(solution)/shard_map/cholesky/custom-call.1 | solution.py:43
  328.1 4.9 custom-call.21
  344.3 5.8 %custom-call.22 = f32[64,64]{1,0:T(8,128)S(1)} custom-call(f32[64,64]{1,0:T(8,128)S(1)} %fusion.176), custom_call_target="Cholesky" | custom-call | tf_op jit(solution)/shard_map/cholesky/custom-call.1 | solution.py:43
  351.5 4.9 custom-call.23
  358.1 5.0 %fusion.120 = f32[448,64]{1,0:T(8,128)S(1)} fusion(f32[64,2048]{1,0:T(8,128)S(1)} %fusion.173, f32[384,2048]{1,0:T(8,128)} %bitcast.306, f32[64,2048]{1,0:T(8,128)} %multiply_bitcast_fusion), kind=kOutput, calls=%fused_computation.130 | convolution fusion | flops 705560576 | bytes 4308992 | tf_op jit(solution)/shard_map/dot_general | solution.py:23
  368.2 6.2 %custom-call.24 = f32[64,64]{1,0:T(8,128)S(1)} custom-call(f32[64,64]{1,0:T(8,128)S(1)} %fusion.172), custom_call_target="Cholesky" | custom-call | tf_op jit(solution)/shard_map/cholesky/custom-call.1 | solution.py:43
  375.8 4.9 custom-call.25
  391.8 5.8 %custom-call.26 = f32[64,64]{1,0:T(8,128)S(1)} custom-call(f32[64,64]{1,0:T(8,128)S(1)} %fusion.168), custom_call_target="Cholesky" | custom-call | tf_op jit(solution)/shard_map/cholesky/custom-call.1 | solution.py:43
  398.9 4.9 custom-call.27
  406.3 5.2 %fusion.118 = f32[448,64]{1,0:T(8,128)S(1)} fusion(f32[64,2048]{1,0:T(8,128)} %fusion.165, f32[384,2048]{1,0:T(8,128)} %bitcast.307, f32[64,2048]{1,0:T(8,128)} %multiply_bitcast_fusion), kind=kOutput, calls=%fused_computation.128 | convolution fusion | flops 705560576 | bytes 4308992 | tf_op jit(solution)/shard_map/dot_general | solution.py:23
  421.7 5.8 %custom-call.28 = f32[64,64]{1,0:T(8,128)S(1)} custom-call(f32[64,64]{1,0:T(8,128)S(1)} %fusion.164), custom_call_target="Cholesky" | custom-call | tf_op jit(solution)/shard_map/cholesky/custom-call.1 | solution.py:43
  428.9 4.9 custom-call.29
  438.1 5.8 %custom-call.30 = f32[64,64]{1,0:T(8,128)S(1)} custom-call(f32[64,64]{1,0:T(8,128)S(1)} %fusion.160), custom_call_target="Cholesky" | custom-call | tf_op jit(solution)/shard_map/cholesky/custom-call.1 | solution.py:43
  445.2 4.9 custom-call.31
  454.6 5.8 %custom-call.32 = f32[64,64]{1,0:T(8,128)S(1)} custom-call(f32[64,64]{1,0:T(8,128)S(1)} %fusion.156), custom_call_target="Cholesky" | custom-call | tf_op jit(solution)/shard_map/cholesky/custom-call.1 | solution.py:43
  461.8 4.9 custom-call.33
  470.9 5.8 %custom-call.34 = f32[64,64]{1,0:T(8,128)S(1)} custom-call(f32[64,64]{1,0:T(8,128)S(1)} %fusion.152), custom_call_target="Cholesky" | custom-call | tf_op jit(solution)/shard_map/cholesky/custom-call.1 | solution.py:43
  478.1 4.9 custom-call.35
  (174 shorter events, 145.0 us)
Async XLA Ops:
  7.2 152.1 %all-gather.4.cloned.1.call-start = ((), (), s32[]{:S(2)}) async-start(), calls=%async_computation.1 | async-start | bytes 4718592 | tf_op jit(solution)/shard_map/all_gather | solution.py:86
  7.9 204.1 %all-gather.6.cloned.1.call-start = ((), (), s32[]{:S(2)}) async-start(), calls=%async_computation.2 | async-start | bytes 4456448 | tf_op jit(solution)/shard_map/all_gather | solution.py:91
  8.6 262.0 %all-gather.8.cloned.1.call-start = ((), (), s32[]{:S(2)}) async-start(), calls=%async_computation.3 | async-start | bytes 4456448 | tf_op jit(solution)/shard_map/all_gather | solution.py:90
  12.9 8.8 %copy-start.15 = (u32[256]{0:T(256)S(1)}, u32[256]{0:T(256)}, u32[]{:S(2)}) copy-start(u32[256]{0:T(256)} %constant.201) | copy-start | bytes 3076
  12.9 21.7 %copy-start.12 = (s32[1,1,1,6]{3,2,1,0:T(1,128)S(1)}, s32[1,1,1,6]{3,2,1,0:T(1,128)}, u32[]{:S(2)}) copy-start(s32[1,1,1,6]{3,2,1,0:T(1,128)} %param.32) | copy-start | bytes 76
  12.9 30.2 %copy-start.14 = (u32[256]{0:T(256)S(1)}, u32[256]{0:T(256)}, u32[]{:S(2)}) copy-start(u32[256]{0:T(256)} %constant.196) | copy-start | bytes 3076
  12.9 31.5 %copy-start.13 = (s32[1,2,1]{1,2,0:T(1,128)S(1)}, s32[1,2,1]{1,2,0:T(1,128)}, u32[]{:S(2)}) copy-start(s32[1,2,1]{1,2,0:T(1,128)} %param.28) | copy-start | bytes 28
  12.9 145.5 %copy-start.11 = (f32[1,1,64,2048]{3,2,1,0:T(8,128)S(1)}, f32[1,1,64,2048]{3,2,1,0:T(8,128)}, u32[]{:S(2)}) copy-start(f32[1,1,64,2048]{3,2,1,0:T(8,128)} %param.24) | copy-start | bytes 1572868
  12.9 146.3 %all-to-all-start = ((bf16[8,1,2,1,64,2048]{5,4,2,3,1,0:T(8,128)(2,1)}), bf16[8,1,2,1,64,2048]{5,4,2,3,1,0:T(8,128)(2,1)}, u32[]{:S(2)}, u32[]{:S(2)}) async-start(bf16[8,1,2,1,64,2048]{5,4,2,3,1,0:T(8,128)(2,1)} %stack.73), calls=%async_computation | async-start | bytes 8388608 | tf_op jit(solution)/shard_map/all_to_all | solution.py:80
  307.0 8.8 %copy-start.2 = (f32[1,1,64,2048]{3,2,1,0:T(8,128)S(1)}, f32[1,1,64,2048]{3,2,1,0:T(8,128)}, u32[]{:S(2)}) copy-start(f32[1,1,64,2048]{3,2,1,0:T(8,128)} %param.25) | copy-start | bytes 1572868
  318.3 0.8 copy-start.7
  333.0 6.1 %copy-start = (f32[6,64,2048]{2,1,0:T(8,128)S(1)}, f32[6,64,2048]{2,1,0:T(8,128)}, u32[]{:S(2)}) copy-start(f32[6,64,2048]{2,1,0:T(8,128)} %constant_dynamic-update-slice_fusion) | copy-start | bytes 9437188
  333.1 6.1 %copy-start.5 = (f32[64,2048]{1,0:T(8,128)S(1)}, f32[64,2048]{1,0:T(8,128)}, u32[]{:S(2)}) copy-start(f32[64,2048]{1,0:T(8,128)} %multiply_bitcast_fusion) | copy-start | bytes 1572868
  341.6 0.8 copy-start.8
  356.4 6.7 %copy-start.3 = (f32[1,1,64,2048]{3,2,1,0:T(8,128)S(1)}, f32[1,1,64,2048]{3,2,1,0:T(8,128)}, u32[]{:S(2)}) copy-start(f32[1,1,64,2048]{3,2,1,0:T(8,128)} %param.25) | copy-start | bytes 1572868
  365.5 0.8 copy-start.9
  380.7 5.9 %copy-start.1 = (f32[6,64,2048]{2,1,0:T(8,128)S(1)}, f32[6,64,2048]{2,1,0:T(8,128)}, u32[]{:S(2)}) copy-start(f32[6,64,2048]{2,1,0:T(8,128)} %constant_dynamic-update-slice_fusion) | copy-start | bytes 9437188
  380.7 5.9 %copy-start.6 = (f32[64,2048]{1,0:T(8,128)S(1)}, f32[64,2048]{1,0:T(8,128)}, u32[]{:S(2)}) copy-start(f32[64,2048]{1,0:T(8,128)} %multiply_bitcast_fusion) | copy-start | bytes 1572868
  389.0 0.8 copy-start.10
  406.3 8.4 %collective-permute-start.1 = (f32[1,64,2048]{2,1,0:T(8,128)}, f32[1,64,2048]{2,1,0:T(8,128)}, u32[]{:S(2)}, u32[]{:S(2)}) collective-permute-start(f32[1,64,2048]{2,1,0:T(8,128)} %bitcast.108), channel_id=1, source_target_pairs={{0,1},{1,0},{2,3},{3,2},{4,5},{5,4},{6,7},{7,6},{8,9},{9,8},{10,11... | collective-permute-start | bytes 1572872 | tf_op jit(solution)/shard_map/ppermute | solution.py:19
  406.3 5.2 %copy-start.4 = (f32[1,1,64,2048]{3,2,1,0:T(8,128)S(1)}, f32[1,1,64,2048]{3,2,1,0:T(8,128)}, u32[]{:S(2)}) copy-start(f32[1,1,64,2048]{3,2,1,0:T(8,128)} %param.25) | copy-start | bytes 1572868
  414.0 5.1 %collective-permute-start = (f32[1,64,2048]{2,1,0:T(8,128)S(1)}, f32[1,64,2048]{2,1,0:T(8,128)S(1)}, u32[]{:S(2)}, u32[]{:S(2)}) collective-permute-start(f32[1,64,2048]{2,1,0:T(8,128)S(1)} %convolution_bitcast_fusion), channel_id=1, source_target_pairs={{0,1},{1,0},{2,3},{3,2},{4,5},{5,4},{6,7},{7,6},{8,9},{9,8},{10,11... | collective-permute-start | bytes 1572872 | tf_op jit(solution)/shard_map/ppermute | solution.py:19
Sparse Core Ops, SparseCore 0:
  9.8 140.4 all-gather.3
  152.7 59.2 all-gather.5
  214.4 56.1 all-gather.7
